TPU v7x, 32 devices: a whole 2x2x4 slice. The times are simulated.
32 devices in a mesh: leaf: 4 (over y, x), row: 2 (over core), col: 4 (over z).
Axes of the slice: x: 2, y: 2, z: 4, core: 2. Of those that a mesh axis runs over, the one named last changes fastest.
Arguments:
- root_inverse: float32 [4096, 4096], P('row', ('leaf', 'col')), may hold values from -48 to 48, as said below
- lower_panel: float32 [4, 4096, 4096], P('leaf', 'row', 'col'), may hold values from -0.375 to 0.375
- panel_mask: int32 [4, 16, 16], P('leaf', 'row', 'col'), may hold values from 0 to 1, as said below
- factor_inverse: float32 [4, 4096, 4096], P('leaf', 'row', 'col'), may hold values from -8 to 8, as said below
Outputs:
- cross_inverse: float32 [4, 4096, 4096], P('leaf', 'row', 'col')
- block_inverse: float32 [4, 4096, 4096], P('leaf', 'row', 'col')
Inputs may be any that keep to these rules, and one draw needn't show every extreme that they name: `panel_mask`: each entry says whether the 256 x 256 block of a child's panel is kept; the share of kept blocks differs from block row to block row. `root_inverse`: symmetric and positive definite. `factor_inverse`: each child's matrix is symmetric and positive definite.
All inputs are finite; a program needn't handle non-finite values.
Results may differ from a plain program's by a relative error of at most 0.0001.
Values sent between devices are 32-bit elements; how exact they have to be, the bound alone decides.
A program may use at most 256 MiB of HBM per device.

v0:
```python
import math

import jax
import jax.numpy as jnp
from jax import lax
from jax.sharding import PartitionSpec as P

BS = 256


def spread_tile(mask_tile):
    return jnp.repeat(jnp.repeat(mask_tile.astype(jnp.float32), BS, axis=1), BS, axis=2)


def block_product(left_block, right_block, present):
    piece_width = left_block.shape[1]
    block_width = math.gcd(piece_width, BS)
    initial = jnp.zeros((left_block.shape[0], right_block.shape[1]), jnp.float32)

    def add_block(block_index, running):
        first_col = block_index * block_width
        block_first = first_col // BS
        block_last = (first_col + block_width - 1) // BS

        def with_block(running_sum):
            left_slice = lax.dynamic_slice_in_dim(left_block, first_col, block_width, 1)
            right_slice = lax.dynamic_slice_in_dim(right_block, first_col, block_width, 0)
            return running_sum + jnp.dot(
                left_slice,
                right_slice,
                precision=lax.Precision.HIGHEST,
                preferred_element_type=jnp.float32,
            )

        def keep_sum(running_sum):
            return running_sum

        needed = present[block_first] + present[block_last] > 0
        return lax.cond(needed, with_block, keep_sum, running)

    return lax.fori_loop(0, piece_width // block_width, add_block, initial)


def per_device(root_inverse, lower_panel, panel_mask, factor_inverse):
    local_pattern = spread_tile(panel_mask)
    local_masked = lower_panel * local_pattern
    gathered_panel, gathered_mask = (
        lax.all_gather(lower_panel, "row", axis=1, tiled=True),
        lax.all_gather(panel_mask, "row", axis=1, tiled=True),
    )
    column_panel = gathered_panel * spread_tile(gathered_mask)
    present = jnp.max(gathered_mask[0], axis=1)
    rows_part = column_panel[0]
    ancestor = block_product(
        lax.all_gather(root_inverse, ("leaf", "col"), axis=1, tiled=True), rows_part, present
    )
    cross_inverse = -(ancestor[None] * local_pattern)
    row_panel = lax.all_gather(local_masked, "col", axis=2, tiled=True)
    left_cols = row_panel[0]
    reduced = lax.psum_scatter(
        lax.dot_general(
            left_cols,
            ancestor,
            (((0,), (0,)), ((), ())),
            precision=lax.Precision.HIGHEST,
            preferred_element_type=jnp.float32,
        ),
        "row",
        scatter_dimension=0,
        tiled=True,
    )
    block_inverse = factor_inverse + reduced[None]
    return (cross_inverse, block_inverse)


def solution(mesh):
    in_specs = (
        P("row", ("leaf", "col")),
        P("leaf", "row", "col"),
        P("leaf", "row", "col"),
        P("leaf", "row", "col"),
    )
    out_specs = (P("leaf", "row", "col"), P("leaf", "row", "col"))
    return jax.shard_map(
        per_device, mesh=mesh, in_specs=in_specs, out_specs=out_specs, check_vma=False
    )
```

profile of v0, /device:TPU:0, one launch (start us, length us, event | category | flops | bytes accessed | tf_op | source)
XLA Modules:
  0.0 1144.6 jit_solution(768674381676361282)
XLA Ops:
  7.2 0.7 all-gather.6.cloned.1.call-update
  8.0 0.7 all-gather.4.cloned.1.call-update
  8.9 4.6 broadcast_in_dim.36
  13.4 11.4 broadcast_in_dim.38
  24.8 15.3 %mul.26 = f32[1,2048,1024]{2,1,0:T(8,128)} multiply(f32[1,2048,1024]{2,1,0:T(8,128)} %param.9, f32[1,2048,1024]{2,1,0:T(8,128)} %broadcast_in_dim.38) | non-fusion elementwise | flops 2097152 | bytes 25165824 | tf_op jit(solution)/shard_map/mul | solution.py:46
  40.3 2.0 all_gather.12
  42.6 8.4 broadcast_in_dim.32
  51.0 21.0 %broadcast_in_dim.33 = f32[1,4096,1024]{2,1,0:T(8,128)} reshape(f32[4096,4,256]{2,1,0:T(4,128)} %broadcast_in_dim.32) | data formatting | bytes 33554432 | tf_op jit(solution)/shard_map/broadcast_in_dim | solution.py:12
  72.4 17.1 %multiply_bitcast_fusion = f32[4096,1024]{1,0:T(8,128)} fusion(f32[1,4096,1024]{2,1,0:T(8,128)} %all-gather.6.cloned.1.call-done, f32[1,4096,1024]{2,1,0:T(8,128)} %broadcast_in_dim.33), kind=kLoop, calls=%fused_computation.6 | loop fusion | flops 4194304 | bytes 50331648 | tf_op jit(solution)/shard_map/squeeze | solution.py:53
  89.5 334.6 %all-gather.4.cloned.1.call-done = f32[2048,4096]{1,0:T(8,128)} async-done(((f32[2048,256]{1,0:T(8,128)}), f32[2048,4096]{1,0:T(8,128)}) %all-gather.4.cloned.1.call-update) | async-done | bytes 33554448 | tf_op jit(solution)/shard_map/all_gather | solution.py:55
  424.1 4.5 broadcast_in_dim.29
  428.5 152.8 %while.21 = (s32[]{:T(128)}, f32[2048,1024]{1,0:T(8,128)}, s32[16]{0:T(128)S(1)}, f32[2048,4096]{1,0:T(8,128)}, f32[4096,1024]{1,0:T(8,128)}, /*index=5*/s32[]{:...) while((s32[]{:T(128)}, f32[2048,1024]{1,0:T(8,128)}, ...), condition=%wide.region_4.5_spmd, body=%wide.region_1.4_spmd.sunk | while | flops 6444548096 | bytes 19924608 | solution.py:41
  428.5 0.7 fusion.8
  430.5 0.7 fusion.8
  432.5 14.0 %conditional.2 = (f32[2048,1024]{1,0:T(8,128)}) conditional(s32[]{:T(128)} %bitcast.20, f32[2048,1024]{1,0:T(8,128)} %get-tuple-element.281, (s32[]{:T(128)}, f32[2048,4096]{1,0:T(8,128)}, f32[4096,1024]{1,0:T(8,128)}, f32[2048,1024]{1,0:T(8,128)}) %tuple.72), branch_computations={%region_2.2_spmd, %region_3.3_spmd} | conditional | flops 6444548096 | bytes 19924010 | solution.py:39
  432.5 14.0 %convolution_add_fusion = f32[2048,1024]{1,0:T(8,128)} fusion(f32[2048,1024]{1,0:T(8,128)} %get-tuple-element.206, f32[2048,4096]{1,0:T(8,128)} %get-tuple-element.207, s32[]{:T(128)S(6)} %select_n.57, f32[4096,1024]{1,0:T(8,128)} %get-tuple-element.209), kind=kOutput, calls=%fused_computation | convolution fusion | flops 6444548096 | bytes 19923968 | tf_op jit(solution)/shard_map/while/body/eval_jaxpr/cond/branch_1_fun/dot_general | solution.py:28
  446.4 0.7 fusion.8
  448.4 0.7 fusion.8
  450.4 12.4 %conditional.2 = (f32[2048,1024]{1,0:T(8,128)}) conditional(s32[]{:T(128)} %bitcast.20, f32[2048,1024]{1,0:T(8,128)} %get-tuple-element.281, (s32[]{:T(128)}, f32[2048,4096]{1,0:T(8,128)}, f32[4096,1024]{1,0:T(8,128)}, f32[2048,1024]{1,0:T(8,128)}) %tuple.72), branch_computations={%region_2.2_spmd, %region_3.3_spmd} | conditional | flops 6444548096 | bytes 19924010 | solution.py:39
  450.4 12.4 %convolution_add_fusion = f32[2048,1024]{1,0:T(8,128)} fusion(f32[2048,1024]{1,0:T(8,128)} %get-tuple-element.206, f32[2048,4096]{1,0:T(8,128)} %get-tuple-element.207, s32[]{:T(128)S(6)} %select_n.57, f32[4096,1024]{1,0:T(8,128)} %get-tuple-element.209), kind=kOutput, calls=%fused_computation | convolution fusion | flops 6444548096 | bytes 19923968 | tf_op jit(solution)/shard_map/while/body/eval_jaxpr/cond/branch_1_fun/dot_general | solution.py:28
  462.8 0.7 fusion.8
  464.8 0.7 fusion.8
  466.7 11.9 %conditional.2 = (f32[2048,1024]{1,0:T(8,128)}) conditional(s32[]{:T(128)} %bitcast.20, f32[2048,1024]{1,0:T(8,128)} %get-tuple-element.281, (s32[]{:T(128)}, f32[2048,4096]{1,0:T(8,128)}, f32[4096,1024]{1,0:T(8,128)}, f32[2048,1024]{1,0:T(8,128)}) %tuple.72), branch_computations={%region_2.2_spmd, %region_3.3_spmd} | conditional | flops 6444548096 | bytes 19924010 | solution.py:39
  466.8 11.9 %convolution_add_fusion = f32[2048,1024]{1,0:T(8,128)} fusion(f32[2048,1024]{1,0:T(8,128)} %get-tuple-element.206, f32[2048,4096]{1,0:T(8,128)} %get-tuple-element.207, s32[]{:T(128)S(6)} %select_n.57, f32[4096,1024]{1,0:T(8,128)} %get-tuple-element.209), kind=kOutput, calls=%fused_computation | convolution fusion | flops 6444548096 | bytes 19923968 | tf_op jit(solution)/shard_map/while/body/eval_jaxpr/cond/branch_1_fun/dot_general | solution.py:28
  478.7 0.7 fusion.8
  480.7 0.7 fusion.8
  482.6 11.9 %conditional.2 = (f32[2048,1024]{1,0:T(8,128)}) conditional(s32[]{:T(128)} %bitcast.20, f32[2048,1024]{1,0:T(8,128)} %get-tuple-element.281, (s32[]{:T(128)}, f32[2048,4096]{1,0:T(8,128)}, f32[4096,1024]{1,0:T(8,128)}, f32[2048,1024]{1,0:T(8,128)}) %tuple.72), branch_computations={%region_2.2_spmd, %region_3.3_spmd} | conditional | flops 6444548096 | bytes 19924010 | solution.py:39
  482.6 11.8 %convolution_add_fusion = f32[2048,1024]{1,0:T(8,128)} fusion(f32[2048,1024]{1,0:T(8,128)} %get-tuple-element.206, f32[2048,4096]{1,0:T(8,128)} %get-tuple-element.207, s32[]{:T(128)S(6)} %select_n.57, f32[4096,1024]{1,0:T(8,128)} %get-tuple-element.209), kind=kOutput, calls=%fused_computation | convolution fusion | flops 6444548096 | bytes 19923968 | tf_op jit(solution)/shard_map/while/body/eval_jaxpr/cond/branch_1_fun/dot_general | solution.py:28
  494.5 0.7 fusion.8
  496.4 11.9 %conditional.2 = (f32[2048,1024]{1,0:T(8,128)}) conditional(s32[]{:T(128)} %bitcast.20, f32[2048,1024]{1,0:T(8,128)} %get-tuple-element.281, (s32[]{:T(128)}, f32[2048,4096]{1,0:T(8,128)}, f32[4096,1024]{1,0:T(8,128)}, f32[2048,1024]{1,0:T(8,128)}) %tuple.72), branch_computations={%region_2.2_spmd, %region_3.3_spmd} | conditional | flops 6444548096 | bytes 19924010 | solution.py:39
  496.4 11.9 %convolution_add_fusion = f32[2048,1024]{1,0:T(8,128)} fusion(f32[2048,1024]{1,0:T(8,128)} %get-tuple-element.206, f32[2048,4096]{1,0:T(8,128)} %get-tuple-element.207, s32[]{:T(128)S(6)} %select_n.57, f32[4096,1024]{1,0:T(8,128)} %get-tuple-element.209), kind=kOutput, calls=%fused_computation | convolution fusion | flops 6444548096 | bytes 19923968 | tf_op jit(solution)/shard_map/while/body/eval_jaxpr/cond/branch_1_fun/dot_general | solution.py:28
  508.3 0.7 fusion.8
  510.2 11.9 %conditional.2 = (f32[2048,1024]{1,0:T(8,128)}) conditional(s32[]{:T(128)} %bitcast.20, f32[2048,1024]{1,0:T(8,128)} %get-tuple-element.281, (s32[]{:T(128)}, f32[2048,4096]{1,0:T(8,128)}, f32[4096,1024]{1,0:T(8,128)}, f32[2048,1024]{1,0:T(8,128)}) %tuple.72), branch_computations={%region_2.2_spmd, %region_3.3_spmd} | conditional | flops 6444548096 | bytes 19924010 | solution.py:39
  510.2 11.9 %convolution_add_fusion = f32[2048,1024]{1,0:T(8,128)} fusion(f32[2048,1024]{1,0:T(8,128)} %get-tuple-element.206, f32[2048,4096]{1,0:T(8,128)} %get-tuple-element.207, s32[]{:T(128)S(6)} %select_n.57, f32[4096,1024]{1,0:T(8,128)} %get-tuple-element.209), kind=kOutput, calls=%fused_computation | convolution fusion | flops 6444548096 | bytes 19923968 | tf_op jit(solution)/shard_map/while/body/eval_jaxpr/cond/branch_1_fun/dot_general | solution.py:28
  524.0 11.9 %conditional.2 = (f32[2048,1024]{1,0:T(8,128)}) conditional(s32[]{:T(128)} %bitcast.20, f32[2048,1024]{1,0:T(8,128)} %get-tuple-element.281, (s32[]{:T(128)}, f32[2048,4096]{1,0:T(8,128)}, f32[4096,1024]{1,0:T(8,128)}, f32[2048,1024]{1,0:T(8,128)}) %tuple.72), branch_computations={%region_2.2_spmd, %region_3.3_spmd} | conditional | flops 6444548096 | bytes 19924010 | solution.py:39
  524.1 11.9 %convolution_add_fusion = f32[2048,1024]{1,0:T(8,128)} fusion(f32[2048,1024]{1,0:T(8,128)} %get-tuple-element.206, f32[2048,4096]{1,0:T(8,128)} %get-tuple-element.207, s32[]{:T(128)S(6)} %select_n.57, f32[4096,1024]{1,0:T(8,128)} %get-tuple-element.209), kind=kOutput, calls=%fused_computation | convolution fusion | flops 6444548096 | bytes 19923968 | tf_op jit(solution)/shard_map/while/body/eval_jaxpr/cond/branch_1_fun/dot_general | solution.py:28
  537.8 11.9 %conditional.2 = (f32[2048,1024]{1,0:T(8,128)}) conditional(s32[]{:T(128)} %bitcast.20, f32[2048,1024]{1,0:T(8,128)} %get-tuple-element.281, (s32[]{:T(128)}, f32[2048,4096]{1,0:T(8,128)}, f32[4096,1024]{1,0:T(8,128)}, f32[2048,1024]{1,0:T(8,128)}) %tuple.72), branch_computations={%region_2.2_spmd, %region_3.3_spmd} | conditional | flops 6444548096 | bytes 19924010 | solution.py:39
  537.8 11.9 %convolution_add_fusion = f32[2048,1024]{1,0:T(8,128)} fusion(f32[2048,1024]{1,0:T(8,128)} %get-tuple-element.206, f32[2048,4096]{1,0:T(8,128)} %get-tuple-element.207, s32[]{:T(128)S(6)} %select_n.57, f32[4096,1024]{1,0:T(8,128)} %get-tuple-element.209), kind=kOutput, calls=%fused_computation | convolution fusion | flops 6444548096 | bytes 19923968 | tf_op jit(solution)/shard_map/while/body/eval_jaxpr/cond/branch_1_fun/dot_general | solution.py:28
  551.7 11.9 %conditional.2 = (f32[2048,1024]{1,0:T(8,128)}) conditional(s32[]{:T(128)} %bitcast.20, f32[2048,1024]{1,0:T(8,128)} %get-tuple-element.281, (s32[]{:T(128)}, f32[2048,4096]{1,0:T(8,128)}, f32[4096,1024]{1,0:T(8,128)}, f32[2048,1024]{1,0:T(8,128)}) %tuple.72), branch_computations={%region_2.2_spmd, %region_3.3_spmd} | conditional | flops 6444548096 | bytes 19924010 | solution.py:39
  551.7 11.9 %convolution_add_fusion = f32[2048,1024]{1,0:T(8,128)} fusion(f32[2048,1024]{1,0:T(8,128)} %get-tuple-element.206, f32[2048,4096]{1,0:T(8,128)} %get-tuple-element.207, s32[]{:T(128)S(6)} %select_n.57, f32[4096,1024]{1,0:T(8,128)} %get-tuple-element.209), kind=kOutput, calls=%fused_computation | convolution fusion | flops 6444548096 | bytes 19923968 | tf_op jit(solution)/shard_map/while/body/eval_jaxpr/cond/branch_1_fun/dot_general | solution.py:28
  565.6 0.7 fusion.8
  567.5 11.9 %conditional.2 = (f32[2048,1024]{1,0:T(8,128)}) conditional(s32[]{:T(128)} %bitcast.20, f32[2048,1024]{1,0:T(8,128)} %get-tuple-element.281, (s32[]{:T(128)}, f32[2048,4096]{1,0:T(8,128)}, f32[4096,1024]{1,0:T(8,128)}, f32[2048,1024]{1,0:T(8,128)}) %tuple.72), branch_computations={%region_2.2_spmd, %region_3.3_spmd} | conditional | flops 6444548096 | bytes 19924010 | solution.py:39
  567.5 11.9 %convolution_add_fusion = f32[2048,1024]{1,0:T(8,128)} fusion(f32[2048,1024]{1,0:T(8,128)} %get-tuple-element.206, f32[2048,4096]{1,0:T(8,128)} %get-tuple-element.207, s32[]{:T(128)S(6)} %select_n.57, f32[4096,1024]{1,0:T(8,128)} %get-tuple-element.209), kind=kOutput, calls=%fused_computation | convolution fusion | flops 6444548096 | bytes 19923968 | tf_op jit(solution)/shard_map/while/body/eval_jaxpr/cond/branch_1_fun/dot_general | solution.py:28
  581.3 403.9 %all-gather.8.cloned.1.call-done = f32[1,2048,4096]{2,1,0:T(8,128)} async-done(((f32[1,2048,1024]{2,1,0:T(8,128)}), f32[1,2048,4096]{2,1,0:T(8,128)}) %all-gather.8.cloned.1.call-update) | async-done | bytes 33554448 | tf_op jit(solution)/shard_map/all_gather | solution.py:58
  985.2 113.4 %fusion.3 = f32[4096,1024]{1,0:T(8,128)} fusion(f32[2048,1024]{1,0:T(8,128)} %get-tuple-element.219, f32[1,2048,4096]{2,1,0:T(8,128)} %all-gather.8.cloned.1.call-done), kind=kOutput, calls=%fused_computation.4 | convolution fusion | flops 103079215104 | bytes 58720256 | tf_op jit(solution)/shard_map/dot_general | solution.py:61
  1098.7 10.5 copy.16
  1109.2 16.7 %negate_bitcast_fusion = f32[1,2048,1024]{2,1,0:T(8,128)} fusion(f32[2048,1024]{1,0:T(8,128)} %get-tuple-element.219, f32[2048,1024]{1,0:T(8,128)} %bitcast.22), kind=kLoop, calls=%fused_computation.8 | loop fusion | flops 4194304 | bytes 25165824 | tf_op jit(solution)/shard_map/neg | solution.py:57
  1125.9 12.1 %bitcast_add_fusion = f32[1,2048,1024]{2,1,0:T(8,128)} fusion(f32[1,2048,1024]{2,1,0:T(8,128)} %param.11, f32[2048,1024]{1,0:T(8,128)} %reduce-scatter.2.cloned.1.call-done), kind=kLoop, calls=%fused_computation.7 | loop fusion | flops 2097152 | bytes 25165824 | tf_op jit(solution)/shard_map/add | solution.py:72
  (30 shorter events, 4.5 us)
Async XLA Ops:
  7.2 1.5 copy-start
  7.2 65.2 %all-gather.6.cloned.1.call-start = ((), (), s32[]{:S(2)}) async-start(), calls=%async_computation.2 | async-start | bytes 25165824 | tf_op jit(solution)/shard_map/all_gather | solution.py:48
  7.9 416.2 %all-gather.4.cloned.1.call-start = ((), (), s32[]{:S(2)}) async-start(), calls=%async_computation.1 | async-start | bytes 35651584 | tf_op jit(solution)/shard_map/all_gather | solution.py:55
  8.7 976.6 %all-gather.8.cloned.1.call-start = ((), (), s32[]{:S(2)}) async-start(), calls=%async_computation.3 | async-start | bytes 41943040 | tf_op jit(solution)/shard_map/all_gather | solution.py:58
  40.2 1085.7 %reduce-scatter.2.cloned.1.call-start = ((), (), s32[]{:S(2)}) async-start(), calls=%async_computation.4 | async-start | bytes 25165824 | tf_op jit(solution)/shard_map/reduce_scatter | solution.py:60
Sparse Core Ops, SparseCore 0:
  9.5 32.7 all-gather.5
  45.1 378.9 all-gather.3
  425.6 559.5 all-gather.7
  1098.8 23.2 reduce-scatter.1
where the time goes:
time: 1150 us; the launch traced here: 1140 us
  waiting for transfers between devices  740 us (64%)
  matrix products  235 us (20%)
  local copies, waits for them, and re-layouts  71.3 us (6%)
  other arithmetic  61.7 us (5%)
  loops' own time  20.9 us (2%)
  between operations  13.8 us (1%)
    all_gather x1, waiting for transfers between devices, per_device(): row_panel = lax.all_gather(local_masked, 'col', axis=2, tiled=True)  404 us
    all_gather x1, waiting for transfers between devices, per_device(): lax.all_gather(root_inverse, ('leaf', 'col'), axis=1, tiled=True)  335 us
    dot_general x10, matrix products, with_block(): jnp.dot(left_slice, right_slice, precision=lax.Precision.HIGHEST, preferr...  121 us
    dot_general x1, matrix products, per_device(): lax.dot_general(left_cols, ancestor, (((0,), (0,)), ((), ())), precision=...  113 us
    broadcast_in_dim x4, local copies, waits for them, and re-layouts, spread_tile(): jnp.repeat(jnp.repeat(mask_tile.astype(jnp.float32), BS, axis=1), BS, axi...  45.3 us
  transfers between devices with their start and end apart: 4, of which 2 were waited for; matrix products, arithmetic and copies ran while one was open for 21% of the time, Pallas kernels for 0%

commit v1 on v0

v1 whole, which is shorter than its diff:
```python
import math

import jax
import jax.numpy as jnp
from jax import lax
from jax.sharding import PartitionSpec as P


BS = 256
CHUNKS = 2


def mul_t(left, right):
    return lax.dot_general(
        left,
        right,
        (((0,), (0,)), ((), ())),
        precision=lax.Precision.HIGH,
        preferred_element_type=jnp.float32,
    )


def pattern_of(mask):
    return jnp.repeat(mask.astype(jnp.float32), BS, axis=1)[:, None, :]


def masked_by(values, pattern):
    rows, cols = values.shape
    return (values.reshape(-1, BS, cols) * pattern).reshape(rows, cols)


def make_per_device(n_row, n_col):
    def per_device(root_inverse, lower_panel, panel_mask, factor_inverse):
        me = lax.axis_index("col")
        row = lax.axis_index("row")
        pattern = pattern_of(panel_mask[0])
        own = masked_by(lower_panel[0], pattern)
        width = own.shape[1]
        ring = [(i, (i + 1) % n_col) for i in range(n_col)]

        root_cols = lax.all_gather(root_inverse, "col", axis=1, tiled=True)
        first, root_cols = lax.optimization_barrier((own, root_cols))
        panels = [first]
        for _ in range(1, n_col // 2):
            panels.append(lax.ppermute(panels[-1], "col", ring))

        column_panel = lax.all_gather(own, "row", axis=0, tiled=True)
        n_rows = root_inverse.shape[0]
        chunks = math.gcd(CHUNKS, n_rows // 8)
        step = n_rows // chunks
        pieces = []
        for c in range(chunks):
            root_rows = lax.all_gather(
                root_cols[c * step : (c + 1) * step], "leaf", axis=1, tiled=True
            )
            if c == 0:
                root_rows, *panels = lax.optimization_barrier((root_rows, *panels))
                if n_col > 1:
                    panels.append(lax.ppermute(panels[-1], "col", ring))
            pieces.append(
                jnp.dot(
                    root_rows,
                    column_panel,
                    precision=lax.Precision.HIGH,
                    preferred_element_type=jnp.float32,
                )
            )
        ancestor = jnp.concatenate(pieces, axis=0)
        cross_inverse = -masked_by(ancestor, pattern)[None]

        partial = jnp.zeros((n_col * width, width), jnp.float32)
        share = width // n_row

        def put(total, block, place, offset=0):
            return lax.dynamic_update_slice_in_dim(total, block, place * width + offset, 0)

        returned = []
        nearer = [d for d in range(1, n_col // 2 + 1) if 2 * d < n_col]
        for d in nearer:
            block = mul_t(ancestor, panels[d])
            summed = lax.psum_scatter(block, "row", scatter_dimension=0, tiled=True)
            back = [(i, (i - d) % n_col) for i in range(n_col)]
            returned.append((d, lax.ppermute(summed, "col", back)))
            partial = put(partial, block.T, lax.rem(me - d + n_col, n_col))
        for d in range(n_col // 2 + 1):
            if d not in nearer:
                block = mul_t(panels[d], ancestor)
                partial = put(partial, block, lax.rem(me - d + n_col, n_col))
        for d, block in returned:
            partial = put(partial, block, lax.rem(me + d, n_col), row * share)

        reduced = lax.psum_scatter(partial, "row", scatter_dimension=0, tiled=True)
        return cross_inverse, factor_inverse + reduced[None]

    return per_device


def solution(mesh):
    in_specs = (
        P("row", ("leaf", "col")),
        P("leaf", "row", "col"),
        P("leaf", "row", "col"),
        P("leaf", "row", "col"),
    )
    out_specs = (P("leaf", "row", "col"), P("leaf", "row", "col"))
    return jax.shard_map(
        make_per_device(mesh.shape["row"], mesh.shape["col"]),
        mesh=mesh,
        in_specs=in_specs,
        out_specs=out_specs,
        check_vma=False,
    )
```

time: 1150 us -> 849 us (0.74)
  waiting for transfers between devices: 740 us -> 633 us
  matrix products: 235 us -> 131 us
  local copies, waits for them, and re-layouts: 71.3 us -> 31.5 us
  other arithmetic: 61.7 us -> 27 us
  loops' own time: 20.9 us -> 0 us
    all_gather x3 -> x4, waiting for transfers between devices: 739 us -> 274 us  [the longest x1 145 us: per_device(): root_cols = lax.all_gather(root_inverse, 'col', axis=1, tiled=True)]
    ppermute x0 -> x3, waiting for transfers between devices: none -> 342 us  [the longest x2 317 us: per_device(): panels.append(lax.ppermute(panels[-1], 'col', ring))]
    dot_general x11 -> x5, matrix products: 235 us -> 131 us  [the longest x3 68.1 us: mul_t(): lax.dot_general(left, right, (((0,), (0,)), ((), ())), precision=lax.Prec...]
    broadcast_in_dim x7 -> x2, local copies, waits for them, and re-layouts: 50 us -> 8.45 us  [the longest x1 8.37 us: per_device(): partial = jnp.zeros((n_col * width, width), jnp.float32)]
    another operation x17 -> x0, loops' own time: 20.9 us -> none  [the longest x1 20.6 us: block_product(): return lax.fori_loop(0, piece_width // block_width, add_block, initial)]
    squeeze x1 -> x0, other arithmetic: 17.1 us -> none  [per_device(): rows_part = column_panel[0]]
    reduce_scatter x1 -> x2, waiting for transfers between devices: 0.01 us -> 14.4 us  [the longest x1 14.4 us: per_device(): reduced = lax.psum_scatter(partial, 'row', scatter_dimension=0, tiled=True)]
  transfers between devices with their start and end apart: 4 -> 9, of which waited for: 2 -> 7; matrix products, arithmetic and copies ran while one was open for 21% -> 14% of each run, Pallas kernels for 0% -> 0%
where the time goes in v1:
time: 849 us; the launch traced here: 842 us
  waiting for transfers between devices  633 us (75%)
  matrix products  131 us (15%)
  local copies, waits for them, and re-layouts  31.5 us (4%)
  other arithmetic  27 us (3%)
  between operations  14.4 us (2%)
    ppermute x2, waiting for transfers between devices, per_device(): panels.append(lax.ppermute(panels[-1], 'col', ring))  317 us
    all_gather x1, waiting for transfers between devices, per_device(): root_cols = lax.all_gather(root_inverse, 'col', axis=1, tiled=True)  145 us
    all_gather x2, waiting for transfers between devices, per_device(): lax.all_gather(root_cols[c * step:(c + 1) * step], 'leaf', axis=1, tiled=...  128 us
    dot_general x3, matrix products, mul_t(): lax.dot_general(left, right, (((0,), (0,)), ((), ())), precision=lax.Prec...  68.1 us
    dot_general x2, matrix products, per_device(): jnp.dot(root_rows, column_panel, precision=lax.Precision.HIGH, preferred_...  63.3 us
    ppermute x1, waiting for transfers between devices, per_device(): returned.append((d, lax.ppermute(summed, 'col', back)))  25.1 us
  transfers between devices with their start and end apart: 9, of which 7 were waited for; matrix products, arithmetic and copies ran while one was open for 14% of the time, Pallas kernels for 0%

profile of v1, /device:TPU:0, one launch (start us, length us, event | category | flops | bytes accessed | tf_op | source)
XLA Modules:
  0.0 842.1 jit_solution(16561463107065529774)
XLA Ops:
  7.2 0.0 all-gather.5.cloned.1.call-start
  7.2 0.7 all-gather.5.cloned.1.call-update
  7.9 0.0 all-gather.7.cloned.1.call-start
  7.9 0.7 convert_bitcast_fusion
  8.6 0.1 broadcast_in_dim.9
  8.7 8.7 %bitcast_multiply_fusion = f32[2048,1024]{1,0:T(8,128)} fusion(f32[1,2048,1024]{2,1,0:T(8,128)} %param.5, f32[8,1024]{1,0:T(8,128)S(1)} %bitcast.26), kind=kLoop, calls=%fused_computation.4 | loop fusion | flops 2097152 | bytes 16809984 | tf_op jit(solution)/shard_map/mul | solution.py:29
  17.4 144.5 %all-gather.5.cloned.1.call-done = f32[2048,1024]{1,0:T(8,128)} async-done(((f32[2048,256]{1,0:T(8,128)}), f32[2048,1024]{1,0:T(8,128)}) %all-gather.5.cloned.1.call-update) | async-done | bytes 8388624 | tf_op jit(solution)/shard_map/all_gather | solution.py:41
  161.9 8.5 %fusion.9 = (f32[1024,1024]{1,0:T(8,128)}, f32[1024,1024]{1,0:T(8,128)}) fusion(f32[2048,1024]{1,0:T(8,128)} %all-gather.5.cloned.1.call-done), kind=kLoop, calls=%fused_computation.16 | loop fusion | bytes 16777216 | tf_op jit(solution)/shard_map/slice | solution.py:54
  170.4 0.0 all-gather.7.cloned.1.call-update
  170.4 0.0 all-gather.9.cloned.1.call-start
  170.5 0.7 all-gather.9.cloned.1.call-update
  171.2 0.0 all-gather.11.cloned.1.call-start
  171.2 0.5 all-gather.11.cloned.1.call-update
  171.7 0.0 reduce-scatter.3.cloned.1.call-start
  171.8 0.1 collective-permute-start
  171.8 184.5 %collective-permute-done = f32[2048,1024]{1,0:T(8,128)} collective-permute-done((f32[2048,1024]{1,0:T(8,128)}, f32[2048,1024]{1,0:T(8,128)}, u32[]{:S(2)}, u32[]{:S(2)}) %collective-permute-start) | collective-permute-done | bytes 8388640 | tf_op jit(solution)/shard_map/ppermute | solution.py:45
  356.3 2.0 all-gather.9.cloned.1.call-done
  358.3 32.4 %fusion.10 = f32[1024,1024]{1,0:T(8,128)} fusion(f32[1024,4096]{1,0:T(8,128)} %all-gather.7.cloned.1.call-done, f32[4096,1024]{1,0:T(8,128)} %all-gather.9.cloned.1.call-done), kind=kOutput, calls=%fused_computation.17 | convolution fusion | flops 25769803776 | bytes 37748736 | tf_op jit(solution)/shard_map/dot_general | solution.py:61
  390.7 127.8 %all-gather.11.cloned.1.call-done = f32[1024,4096]{1,0:T(8,128)} async-done(((f32[1024,1024]{1,0:T(8,128)}), f32[1024,4096]{1,0:T(8,128)}) %all-gather.11.cloned.1.call-update) | async-done | bytes 16777232 | tf_op jit(solution)/shard_map/all_gather | solution.py:53
  518.5 30.9 %fusion.11 = f32[1024,1024]{1,0:T(8,128)S(1)} fusion(f32[1024,4096]{1,0:T(8,128)} %all-gather.11.cloned.1.call-done, f32[4096,1024]{1,0:T(8,128)} %all-gather.9.cloned.1.call-done), kind=kOutput, calls=%fused_computation.18 | convolution fusion | flops 25769803776 | bytes 37748736 | tf_op jit(solution)/shard_map/dot_general | solution.py:61
  549.4 0.0 copy-start.4
  549.4 2.0 copy-done.4
  551.4 0.0 copy-done.1
  551.4 17.5 %fusion.3 = f32[1024,1024]{1,0:T(8,128)} fusion(f32[2048,1024]{1,0:T(8,128)} %collective-permute-done, f32[1024,1024]{1,0:T(8,128)S(1)} %fusion.11, f32[1024,1024]{1,0:T(8,128)S(1)} %copy-done.1), kind=kOutput, calls=%fused_computation.7 | convolution fusion | flops 12886999040 | bytes 20971520 | tf_op jit(solution)/shard_map/dot_general | solution.py:14
  568.9 0.0 reduce-scatter.3.cloned.1.call-update
  568.9 0.0 reduce-scatter.5.cloned.1.call-start
  569.0 1.5 collective-permute-start.1
  570.5 5.4 copy.6
  575.9 8.4 broadcast_in_dim.10
  584.3 0.0 copy-done
  584.3 2.3 constant_dynamic-update-slice_fusion.1
  586.5 3.0 collective-permute-start.2
  589.6 32.2 %fusion.4 = f32[4096,1024]{1,0:T(8,128)} fusion(f32[4096,1024]{1,0:T(8,128)} %constant_dynamic-update-slice_fusion.1, s32[]{:T(128)S(6)} %select_n.13, f32[2048,1024]{1,0:T(8,128)} %bitcast_multiply_fusion, f32[1024,1024]{1,0:T(8,128)} %copy-done.4, f32[1024,1024]{1,0:T(8,128)} %fusion.10), kind=kOutput, calls=%fused_computation.8 | convolution fusion | flops 12886999040 | bytes 20971524 | tf_op jit(solution)/shard_map/dot_general | solution.py:14
  621.8 132.7 %collective-permute-done.1 = f32[2048,1024]{1,0:T(8,128)} collective-permute-done((f32[2048,1024]{1,0:T(8,128)}, f32[2048,1024]{1,0:T(8,128)}, u32[]{:S(2)}, u32[]{:S(2)}) %collective-permute-start.1) | collective-permute-done | bytes 8388640 | tf_op jit(solution)/shard_map/ppermute | solution.py:59
  754.5 0.0 copy-done.2
  754.5 0.0 copy-done.5
  754.5 18.4 %fusion.5 = f32[4096,1024]{1,0:T(8,128)} fusion(f32[4096,1024]{1,0:T(8,128)} %fusion.4, s32[]{:T(128)S(6)} %select_n.14, f32[2048,1024]{1,0:T(8,128)} %collective-permute-done.1, f32[1024,1024]{1,0:T(8,128)S(1)} %copy-done.5, f32[1024,1024]{1,0:T(8,128)S(1)} %copy-done.2), kind=kOutput, calls=%fused_computation.9 | convolution fusion | flops 12886999040 | bytes 20971524 | tf_op jit(solution)/shard_map/dot_general | solution.py:14
  772.9 25.1 %collective-permute-done.2 = f32[512,1024]{1,0:T(8,128)S(1)} collective-permute-done((f32[512,1024]{1,0:T(8,128)}, f32[512,1024]{1,0:T(8,128)S(1)}, u32[]{:S(2)}, u32[]{:S(2)}) %collective-permute-start.2) | collective-permute-done | bytes 2097184 | tf_op jit(solution)/shard_map/ppermute | solution.py:83
  798.0 1.5 constant_dynamic-update-slice_fusion
  799.5 0.0 reduce-scatter.5.cloned.1.call-update
  799.5 0.0 copy-start.3
  799.5 0.0 copy-start.6
  799.6 1.1 mul.45
  800.6 1.1 copy-done.3
  801.7 1.3 copy-done.6
  803.0 5.5 fusion
  808.5 14.4 %reduce-scatter.5.cloned.1.call-done = f32[2048,1024]{1,0:T(8,128)} async-done(((f32[4096,1024]{1,0:T(8,128)}), f32[2048,1024]{1,0:T(8,128)}) %reduce-scatter.5.cloned.1.call-update) | async-done | bytes 8388624 | tf_op jit(solution)/shard_map/reduce_scatter | solution.py:92
  822.9 12.1 %bitcast_add_fusion = f32[1,2048,1024]{2,1,0:T(8,128)} fusion(f32[1,2048,1024]{2,1,0:T(8,128)} %param.7, f32[2048,1024]{1,0:T(8,128)} %reduce-scatter.5.cloned.1.call-done), kind=kLoop, calls=%fused_computation.3 | loop fusion | flops 2097152 | bytes 25165824 | tf_op jit(solution)/shard_map/add | solution.py:93
  (6 shorter events, 0.0 us)
Async XLA Ops:
  7.2 154.7 %all-gather.5.cloned.1.call-start = ((), (), s32[]{:S(2)}) async-start(), calls=%async_computation.2 | async-start | bytes 10485760 | tf_op jit(solution)/shard_map/all_gather | solution.py:41
  7.9 348.4 %all-gather.7.cloned.1.call-start = ((), (), s32[]{:S(2)}) async-start(), calls=%async_computation.3 | async-start | bytes 20971520 | tf_op jit(solution)/shard_map/all_gather | solution.py:53
  170.4 187.9 %all-gather.9.cloned.1.call-start = ((), (), s32[]{:S(2)}) async-start(), calls=%async_computation.4 | async-start | bytes 25165824 | tf_op jit(solution)/shard_map/all_gather | solution.py:47
  171.2 347.3 %all-gather.11.cloned.1.call-start = ((), (), s32[]{:S(2)}) async-start(), calls=%async_computation.5 | async-start | bytes 20971520 | tf_op jit(solution)/shard_map/all_gather | solution.py:53
  171.7 414.8 %reduce-scatter.3.cloned.1.call-start = ((), (), s32[]{:S(2)}) async-start(), calls=%async_computation.6 | async-start | bytes 6291456 | tf_op jit(solution)/shard_map/reduce_scatter | solution.py:81
  171.8 184.5 %collective-permute-start = (f32[2048,1024]{1,0:T(8,128)}, f32[2048,1024]{1,0:T(8,128)}, u32[]{:S(2)}, u32[]{:S(2)}) collective-permute-start(f32[2048,1024]{1,0:T(8,128)} %bitcast_multiply_fusion), channel_id=1, source_target_pairs={{0,1},{1,2},{2,3},{3,0},{4,5},{5,6},{6,7},{7,4},{8,9},{9,10},{10,1... | collective-permute-start | bytes 25165832 | tf_op jit(solution)/shard_map/ppermute | solution.py:45
  518.5 33.0 %copy-start.1 = (f32[1024,1024]{1,0:T(8,128)S(1)}, f32[1024,1024]{1,0:T(8,128)}, u32[]{:S(2)}) copy-start(f32[1024,1024]{1,0:T(8,128)} %fusion.10) | copy-start | bytes 12582916
  549.4 2.0 copy-start.4
  568.9 254.0 %reduce-scatter.5.cloned.1.call-start = ((), (), s32[]{:S(2)}) async-start(), calls=%async_computation.7 | async-start | bytes 25165824 | tf_op jit(solution)/shard_map/reduce_scatter | solution.py:92
  569.0 185.5 %collective-permute-start.1 = (f32[2048,1024]{1,0:T(8,128)}, f32[2048,1024]{1,0:T(8,128)}, u32[]{:S(2)}, u32[]{:S(2)}) collective-permute-start(f32[2048,1024]{1,0:T(8,128)} %collective-permute-done), channel_id=1, source_target_pairs={{0,1},{1,2},{2,3},{3,0},{4,5},{5,6},{6,7},{7,4},{8,9},{9,10},{10,1... | collective-permute-start | bytes 25165832 | tf_op jit(solution)/shard_map/ppermute | solution.py:59
  575.9 8.4 copy-start
  586.5 168.0 %copy-start.2 = (f32[1024,1024]{1,0:T(8,128)S(1)}, f32[1024,1024]{1,0:T(8,128)}, u32[]{:S(2)}) copy-start(f32[1024,1024]{1,0:T(8,128)} %fusion.10) | copy-start | bytes 12582916
  586.5 168.0 %copy-start.5 = (f32[1024,1024]{1,0:T(8,128)S(1)}, f32[1024,1024]{1,0:T(8,128)}, u32[]{:S(2)}) copy-start(f32[1024,1024]{1,0:T(8,128)} %copy-done.4) | copy-start | bytes 12582916
  586.5 211.5 %collective-permute-start.2 = (f32[512,1024]{1,0:T(8,128)}, f32[512,1024]{1,0:T(8,128)S(1)}, u32[]{:S(2)}, u32[]{:S(2)}) collective-permute-start(f32[512,1024]{1,0:T(8,128)} %reduce-scatter.3.cloned.1.call-done), channel_id=1, source_target_pairs={{0,3},{1,0},{2,1},{3,2},{4,7},{5,4},{6,5},{7,6},{8,11},{9,8},{10,9... | collective-permute-start | bytes 6291464 | tf_op jit(solution)/shard_map/ppermute | solution.py:83
  799.5 2.2 copy-start.3
  799.5 3.5 copy-start.6
Sparse Core Ops, SparseCore 0:
  9.5 152.3 all-gather.4
  170.5 155.4 all-gather.6
  328.2 30.0 all-gather.8
  360.0 158.4 all-gather.10
  569.1 12.0 reduce-scatter.2
  799.6 23.2 reduce-scatter.4

commit v2 on v1

--- a/solution.py
+++ b/solution.py
@@ -49,6 +49,8 @@
         chunks = math.gcd(CHUNKS, n_rows // 8)
         step = n_rows // chunks
         pieces = []
+        nearer = [d for d in range(1, n_col // 2 + 1) if 2 * d < n_col]
+        blocks = {}
         for c in range(chunks):
             root_rows = lax.all_gather(
                 root_cols[c * step : (c + 1) * step], "leaf", axis=1, tiled=True
@@ -65,6 +67,11 @@
                     preferred_element_type=jnp.float32,
                 )
             )
+            for d in range(max(n_col // 2, 1)):
+                rows = panels[d][c * step : (c + 1) * step]
+                pair = (pieces[-1], rows) if d in nearer else (rows, pieces[-1])
+                term = mul_t(*pair)
+                blocks[d] = blocks[d] + term if c else lax.optimization_barrier(term)
         ancestor = jnp.concatenate(pieces, axis=0)
         cross_inverse = -masked_by(ancestor, pattern)[None]
 
@@ -75,16 +82,16 @@
             return lax.dynamic_update_slice_in_dim(total, block, place * width + offset, 0)
 
         returned = []
-        nearer = [d for d in range(1, n_col // 2 + 1) if 2 * d < n_col]
         for d in nearer:
-            block = mul_t(ancestor, panels[d])
-            summed = lax.psum_scatter(block, "row", scatter_dimension=0, tiled=True)
+            if d not in blocks:
+                blocks[d] = mul_t(ancestor, panels[d])
+            summed = lax.psum_scatter(blocks[d], "row", scatter_dimension=0, tiled=True)
             back = [(i, (i - d) % n_col) for i in range(n_col)]
             returned.append((d, lax.ppermute(summed, "col", back)))
-            partial = put(partial, block.T, lax.rem(me - d + n_col, n_col))
+            partial = put(partial, blocks[d].T, lax.rem(me - d + n_col, n_col))
         for d in range(n_col // 2 + 1):
             if d not in nearer:
-                block = mul_t(panels[d], ancestor)
+                block = blocks[d] if d in blocks else mul_t(panels[d], ancestor)
                 partial = put(partial, block, lax.rem(me - d + n_col, n_col))
         for d, block in returned:
             partial = put(partial, block, lax.rem(me + d, n_col), row * share)

time: 849 us -> 840 us (0.989)
  other arithmetic: 27 us -> 37.4 us
  matrix products: 131 us -> 122 us
    all_gather x2, waiting for transfers between devices: 128 us -> 118 us  [per_device(): lax.all_gather(root_cols[c * step:(c + 1) * step], 'leaf', axis=1, tiled=...]
    dot_general x3 -> x5, matrix products: 68.1 us -> 59.9 us  [mul_t(): lax.dot_general(left, right, (((0,), (0,)), ((), ())), precision=lax.Prec...]
where the time goes in v2:
time: 840 us; the launch traced here: 837 us
  waiting for transfers between devices  626 us (75%)
  matrix products  122 us (15%)
  other arithmetic  37.4 us (4%)
  local copies, waits for them, and re-layouts  32.9 us (4%)
  between operations  14.4 us (2%)
    ppermute x2, waiting for transfers between devices, per_device(): panels.append(lax.ppermute(panels[-1], 'col', ring))  321 us
    all_gather x1, waiting for transfers between devices, per_device(): root_cols = lax.all_gather(root_inverse, 'col', axis=1, tiled=True)  145 us
    all_gather x2, waiting for transfers between devices, per_device(): lax.all_gather(root_cols[c * step:(c + 1) * step], 'leaf', axis=1, tiled=...  118 us
    dot_general x2, matrix products, per_device(): jnp.dot(root_rows, column_panel, precision=lax.Precision.HIGH, preferred_...  62.3 us
    dot_general x5, matrix products, mul_t(): lax.dot_general(left, right, (((0,), (0,)), ((), ())), precision=lax.Prec...  59.9 us
    ppermute x1, waiting for transfers between devices, per_device(): returned.append((d, lax.ppermute(summed, 'col', back)))  25.1 us
  transfers between devices with their start and end apart: 9, of which 7 were waited for; matrix products, arithmetic and copies ran while one was open for 14% of the time, Pallas kernels for 0%

profile of v2, /device:TPU:0, one launch (start us, length us, event | category | flops | bytes accessed | tf_op | source)
XLA Modules:
  0.0 837.2 jit_solution(12476762155377888690)
XLA Ops:
  7.2 0.0 all-gather.5.cloned.1.call-start
  7.2 0.7 all-gather.5.cloned.1.call-update
  7.9 0.0 all-gather.7.cloned.1.call-start
  7.9 0.7 convert_bitcast_fusion
  8.6 0.1 broadcast_in_dim.9
  8.7 8.7 %bitcast_multiply_fusion = f32[2048,1024]{1,0:T(8,128)} fusion(f32[1,2048,1024]{2,1,0:T(8,128)} %param.5, f32[8,1024]{1,0:T(8,128)S(1)} %bitcast.30), kind=kLoop, calls=%fused_computation.7 | loop fusion | flops 2097152 | bytes 16809984 | tf_op jit(solution)/shard_map/mul | solution.py:29
  17.4 144.5 %all-gather.5.cloned.1.call-done = f32[2048,1024]{1,0:T(8,128)} async-done(((f32[2048,256]{1,0:T(8,128)}), f32[2048,1024]{1,0:T(8,128)}) %all-gather.5.cloned.1.call-update) | async-done | bytes 8388624 | tf_op jit(solution)/shard_map/all_gather | solution.py:41
  161.9 8.4 %fusion.17 = (f32[1024,1024]{1,0:T(8,128)}, f32[1024,1024]{1,0:T(8,128)}) fusion(f32[2048,1024]{1,0:T(8,128)} %all-gather.5.cloned.1.call-done), kind=kLoop, calls=%fused_computation.22 | loop fusion | bytes 16777216 | tf_op jit(solution)/shard_map/slice | solution.py:56
  170.4 0.0 all-gather.7.cloned.1.call-update
  170.4 0.0 all-gather.9.cloned.1.call-start
  170.4 0.7 all-gather.9.cloned.1.call-update
  171.1 0.0 all-gather.11.cloned.1.call-start
  171.2 0.5 all-gather.11.cloned.1.call-update
  171.7 0.0 reduce-scatter.3.cloned.1.call-start
  171.7 0.4 collective-permute-start
  172.1 184.5 %collective-permute-done = f32[2048,1024]{1,0:T(8,128)} collective-permute-done((f32[2048,1024]{1,0:T(8,128)}, f32[2048,1024]{1,0:T(8,128)}, u32[]{:S(2)}, u32[]{:S(2)}) %collective-permute-start) | collective-permute-done | bytes 8388640 | tf_op jit(solution)/shard_map/ppermute | solution.py:45
  356.6 1.7 all-gather.9.cloned.1.call-done
  358.2 30.5 %fusion.18 = f32[1024,1024]{1,0:T(8,128)S(1)} fusion(f32[1024,4096]{1,0:T(8,128)} %all-gather.7.cloned.1.call-done, f32[4096,1024]{1,0:T(8,128)} %all-gather.9.cloned.1.call-done), kind=kOutput, calls=%fused_computation.23 | convolution fusion | flops 25769803776 | bytes 37748736 | tf_op jit(solution)/shard_map/dot_general | solution.py:63
  388.8 2.1 copy-done.2
  390.9 9.9 %fusion.11 = f32[1024,1024]{1,0:T(8,128)} fusion(f32[1024,1024]{1,0:T(8,128)S(1)} %fusion.18, f32[2048,1024]{1,0:T(8,128)} %collective-permute-done), kind=kOutput, calls=%fused_computation.15 | convolution fusion | flops 6442450944 | bytes 12582912 | tf_op jit(solution)/shard_map/dot_general | solution.py:14
  400.8 117.6 %all-gather.11.cloned.1.call-done = f32[1024,4096]{1,0:T(8,128)} async-done(((f32[1024,1024]{1,0:T(8,128)}), f32[1024,4096]{1,0:T(8,128)}) %all-gather.11.cloned.1.call-update) | async-done | bytes 16777232 | tf_op jit(solution)/shard_map/all_gather | solution.py:55
  518.4 31.8 %fusion.19 = f32[1024,1024]{1,0:T(8,128)S(1)} fusion(f32[1024,4096]{1,0:T(8,128)} %all-gather.11.cloned.1.call-done, f32[4096,1024]{1,0:T(8,128)} %all-gather.9.cloned.1.call-done), kind=kOutput, calls=%fused_computation.24 | convolution fusion | flops 25769803776 | bytes 37748736 | tf_op jit(solution)/shard_map/dot_general | solution.py:63
  550.2 0.0 copy-start.5
  550.2 10.7 %fusion.9 = f32[1024,1024]{1,0:T(8,128)S(1)} fusion(f32[1024,1024]{1,0:T(8,128)S(1)} %fusion.19, f32[2048,1024]{1,0:T(8,128)} %collective-permute-done), kind=kOutput, calls=%fused_computation.13 | convolution fusion | flops 6442450944 | bytes 12582912 | tf_op jit(solution)/shard_map/dot_general | solution.py:14
  561.0 2.9 add.46
  563.9 0.0 reduce-scatter.3.cloned.1.call-update
  563.9 0.0 reduce-scatter.5.cloned.1.call-start
  564.0 1.5 collective-permute-start.1
  565.5 5.6 copy.6
  571.1 12.4 %fusion.7 = f32[1024,1024]{1,0:T(8,128)} fusion(f32[1024,1024]{1,0:T(8,128)} %copy-done.2, f32[2048,1024]{1,0:T(8,128)} %bitcast_multiply_fusion), kind=kOutput, calls=%fused_computation.11 | convolution fusion | flops 6442450944 | bytes 12582912 | tf_op jit(solution)/shard_map/dot_general | solution.py:14
  583.5 8.1 broadcast_in_dim.10
  591.7 2.4 constant_dynamic-update-slice_fusion.1
  594.1 1.3 copy-done.6
  595.4 8.5 %fusion.5 = f32[1024,1024]{1,0:T(8,128)} fusion(f32[1024,1024]{1,0:T(8,128)S(1)} %copy-done.6, f32[2048,1024]{1,0:T(8,128)S(1)} %bitcast.27), kind=kOutput, calls=%fused_computation.9 | convolution fusion | flops 6442450944 | bytes 12582912 | tf_op jit(solution)/shard_map/dot_general | solution.py:14
  603.8 1.5 collective-permute-start.2
  605.4 7.5 add_dynamic-update-slice_fusion
  612.8 136.7 %collective-permute-done.1 = f32[2048,1024]{1,0:T(8,128)} collective-permute-done((f32[2048,1024]{1,0:T(8,128)}, f32[2048,1024]{1,0:T(8,128)}, u32[]{:S(2)}, u32[]{:S(2)}) %collective-permute-start.1) | collective-permute-done | bytes 8388640 | tf_op jit(solution)/shard_map/ppermute | solution.py:61
  749.5 18.4 %fusion.13 = f32[4096,1024]{1,0:T(8,128)} fusion(f32[4096,1024]{1,0:T(8,128)} %add_dynamic-update-slice_fusion, s32[]{:T(128)S(6)} %select_n.14, f32[2048,1024]{1,0:T(8,128)} %collective-permute-done.1, f32[1024,1024]{1,0:T(8,128)S(1)} %copy-done.7, f32[1024,1024]{1,0:T(8,128)S(1)} %copy-done.3), kind=kOutput, calls=%fused_computation.17 | convolution fusion | flops 12886999040 | bytes 20971524 | tf_op jit(solution)/shard_map/dot_general | solution.py:14
  767.9 25.1 %collective-permute-done.2 = f32[512,1024]{1,0:T(8,128)S(1)} collective-permute-done((f32[512,1024]{1,0:T(8,128)}, f32[512,1024]{1,0:T(8,128)S(1)}, u32[]{:S(2)}, u32[]{:S(2)}) %collective-permute-start.2) | collective-permute-done | bytes 2097184 | tf_op jit(solution)/shard_map/ppermute | solution.py:90
  793.0 1.5 constant_dynamic-update-slice_fusion
  794.5 0.0 reduce-scatter.5.cloned.1.call-update
  794.6 0.0 copy-start.8
  794.6 1.1 mul.45
  795.6 1.1 copy-done.4
  796.7 1.3 copy-done.8
  798.0 5.5 fusion
  803.5 14.4 %reduce-scatter.5.cloned.1.call-done = f32[2048,1024]{1,0:T(8,128)} async-done(((f32[4096,1024]{1,0:T(8,128)}), f32[2048,1024]{1,0:T(8,128)}) %reduce-scatter.5.cloned.1.call-update) | async-done | bytes 8388624 | tf_op jit(solution)/shard_map/reduce_scatter | solution.py:99
  817.9 12.1 %bitcast_add_fusion = f32[1,2048,1024]{2,1,0:T(8,128)} fusion(f32[1,2048,1024]{2,1,0:T(8,128)} %param.7, f32[2048,1024]{1,0:T(8,128)} %reduce-scatter.5.cloned.1.call-done), kind=kLoop, calls=%fused_computation.6 | loop fusion | flops 2097152 | bytes 25165824 | tf_op jit(solution)/shard_map/add | solution.py:100
  (19 shorter events, 0.0 us)
Async XLA Ops:
  7.2 154.7 %all-gather.5.cloned.1.call-start = ((), (), s32[]{:S(2)}) async-start(), calls=%async_computation.2 | async-start | bytes 10485760 | tf_op jit(solution)/shard_map/all_gather | solution.py:41
  7.9 348.7 %all-gather.7.cloned.1.call-start = ((), (), s32[]{:S(2)}) async-start(), calls=%async_computation.3 | async-start | bytes 20971520 | tf_op jit(solution)/shard_map/all_gather | solution.py:55
  170.4 187.9 %all-gather.9.cloned.1.call-start = ((), (), s32[]{:S(2)}) async-start(), calls=%async_computation.4 | async-start | bytes 25165824 | tf_op jit(solution)/shard_map/all_gather | solution.py:47
  171.1 347.3 %all-gather.11.cloned.1.call-start = ((), (), s32[]{:S(2)}) async-start(), calls=%async_computation.5 | async-start | bytes 20971520 | tf_op jit(solution)/shard_map/all_gather | solution.py:55
  171.7 432.1 %reduce-scatter.3.cloned.1.call-start = ((), (), s32[]{:S(2)}) async-start(), calls=%async_computation.6 | async-start | bytes 6291456 | tf_op jit(solution)/shard_map/reduce_scatter | solution.py:88
  171.7 184.8 %collective-permute-start = (f32[2048,1024]{1,0:T(8,128)}, f32[2048,1024]{1,0:T(8,128)}, u32[]{:S(2)}, u32[]{:S(2)}) collective-permute-start(f32[2048,1024]{1,0:T(8,128)} %bitcast_multiply_fusion), channel_id=1, source_target_pairs={{0,1},{1,2},{2,3},{3,0},{4,5},{5,6},{6,7},{7,4},{8,9},{9,10},{10,1... | collective-permute-start | bytes 25165832 | tf_op jit(solution)/shard_map/ppermute | solution.py:45
  388.8 2.1 copy-start.2
  550.2 10.7 %copy-start.5 = (f32[1024,1024]{1,0:T(8,128)}, f32[1024,1024]{1,0:T(8,128)S(1)}, u32[]{:S(2)}) copy-start(f32[1024,1024]{1,0:T(8,128)S(1)} %fusion.19) | copy-start | bytes 12582916
  550.2 10.7 %copy-start.1 = (f32[1024,1024]{1,0:T(8,128)S(1)}, f32[1024,1024]{1,0:T(8,128)}, u32[]{:S(2)}) copy-start(f32[1024,1024]{1,0:T(8,128)} %fusion.11) | copy-start | bytes 12582916
  563.9 254.0 %reduce-scatter.5.cloned.1.call-start = ((), (), s32[]{:S(2)}) async-start(), calls=%async_computation.7 | async-start | bytes 25165824 | tf_op jit(solution)/shard_map/reduce_scatter | solution.py:99
  564.0 185.5 %collective-permute-start.1 = (f32[2048,1024]{1,0:T(8,128)}, f32[2048,1024]{1,0:T(8,128)}, u32[]{:S(2)}, u32[]{:S(2)}) collective-permute-start(f32[2048,1024]{1,0:T(8,128)} %collective-permute-done), channel_id=1, source_target_pairs={{0,1},{1,2},{2,3},{3,0},{4,5},{5,6},{6,7},{7,4},{8,9},{9,10},{10,1... | collective-permute-start | bytes 25165832 | tf_op jit(solution)/shard_map/ppermute | solution.py:61
  571.1 23.0 %slice-start = ((s8[8388608]{0:T(1024)(128)(4,1)}), s8[4194304]{0:T(1024)(128)(4,1)S(1)}, s32[]{:S(2)}) async-start(s8[8388608]{0:T(1024)(128)(4,1)} %bitcast.26), calls=%async_computation.8 | async-start | bytes 8388608
  583.5 8.1 copy-start
  583.5 10.6 %slice-start.1 = ((s8[8388608]{0:T(1024)(128)(4,1)}), s8[4194304]{0:T(1024)(128)(4,1)S(1)}, s32[]{:S(2)}) async-start(s8[8388608]{0:T(1024)(128)(4,1)} %bitcast.26), calls=%async_computation.9 | async-start | bytes 8388608
  591.7 3.7 copy-start.6
  603.8 145.7 %copy-start.3 = (f32[1024,1024]{1,0:T(8,128)S(1)}, f32[1024,1024]{1,0:T(8,128)}, u32[]{:S(2)}) copy-start(f32[1024,1024]{1,0:T(8,128)} %copy-done.2) | copy-start | bytes 12582916
  603.8 145.7 %copy-start.7 = (f32[1024,1024]{1,0:T(8,128)S(1)}, f32[1024,1024]{1,0:T(8,128)}, u32[]{:S(2)}) copy-start(f32[1024,1024]{1,0:T(8,128)} %copy-done.5) | copy-start | bytes 12582916
  603.8 189.2 %collective-permute-start.2 = (f32[512,1024]{1,0:T(8,128)}, f32[512,1024]{1,0:T(8,128)S(1)}, u32[]{:S(2)}, u32[]{:S(2)}) collective-permute-start(f32[512,1024]{1,0:T(8,128)} %reduce-scatter.3.cloned.1.call-done), channel_id=1, source_target_pairs={{0,3},{1,0},{2,1},{3,2},{4,7},{5,4},{6,5},{7,6},{8,11},{9,8},{10,9... | collective-permute-start | bytes 6291464 | tf_op jit(solution)/shard_map/ppermute | solution.py:90
  794.5 2.2 copy-start.4
  794.6 3.5 copy-start.8
Sparse Core Ops, SparseCore 0:
  9.5 152.3 all-gather.4
  170.5 155.4 all-gather.6
  328.1 30.0 all-gather.8
  359.9 158.4 all-gather.10
  564.0 12.0 reduce-scatter.2
  794.7 23.2 reduce-scatter.4
